TPU v7x, 256 devices: a whole 4x4x8 slice. The times are simulated.
256 devices in a mesh: row: 32 (over z, y), col: 8 (over x, core).
Axes of the slice: x: 4, y: 4, z: 8, core: 2. Of those that a mesh axis runs over, the one named last changes fastest.
Arguments:
- expression: bfloat16 [32768, 1024], P(('row', 'col')), as said below
- power_order: int32 [20], replicated, may hold values from 0 to 19, each once
Outputs:
- log_conn: float32 [32768, 20], P(('row', 'col'))
- fit: float32 [20], replicated
- slope: float32 [20], replicated
Inputs may be any that keep to these rules, and one draw needn't show every extreme that they name: `expression`: each gene's row has mean zero and unit variance over the samples, up to rounding.
All inputs are finite; a program needn't handle non-finite values.
Results may differ from a plain program's by a relative error of at most 0.0029.
Values may be sent and summed in bfloat16 or wider, within the bound.
A program may use at most 64 MiB of HBM per device.

v0:
```python
import functools
import math

import jax
import jax.numpy as jnp
from jax import lax
from jax.sharding import Mesh
from jax.sharding import PartitionSpec as P

ROW = ("row_0", "row_1")
COL = ("col_0", "col_1")
ROW_COL = ("row_0", "row_1", "col_0", "col_1")


def from_everyone(x, axis):
    copies = jnp.broadcast_to(x, (lax.axis_size(axis), *x.shape))
    return lax.all_to_all(copies, axis, split_axis=0, concat_axis=0, tiled=True)


def in_order(tiles, dim):
    tiles = jnp.moveaxis(tiles, 0, dim)
    lengths = tiles.shape
    return tiles.reshape(*lengths[:dim], lengths[dim] * lengths[dim + 1], *lengths[dim + 2 :])


def gather_directly(x, axis, dim):
    tiles = from_everyone(x, axis)
    return in_order(tiles, dim)


def cut_along(x, dim, devices):
    lengths = x.shape
    tiles = x.reshape(*lengths[:dim], devices, lengths[dim] // devices, *lengths[dim + 1 :])
    return jnp.moveaxis(tiles, dim, 0)


def sum_at_owner(x, axis, dim):
    tiles = cut_along(x, dim, lax.axis_size(axis))
    arrived = lax.all_to_all(tiles, axis, split_axis=0, concat_axis=0, tiled=True)
    return arrived.sum(axis=0)


def over_axes(x, axes):
    return functools.reduce(lax.psum, axes, x)


def power_sums(rows, partners, samples, powers):
    corr = (
        lax.dot_general(
            rows, partners, (((1,), (1,)), ((), ())), preferred_element_type=jnp.float32
        )
        / samples
    )
    magnitude = jnp.abs(corr)
    current = magnitude
    sums = []
    for power in range(powers):
        sums.append(jnp.sum(current, axis=1))
        current = current * magnitude
    return jnp.stack(sums, axis=1)


def scale_free_fit(hist, log_total, bins):
    centers = jnp.arange(bins, dtype=jnp.float32) * (log_total / (bins - 1))
    weight_sum = jnp.sum(hist, axis=1, keepdims=True)
    ylog = jnp.log(hist + 1.0) - log_total
    xmean = jnp.sum(hist * centers[None, :], axis=1, keepdims=True) / weight_sum
    ymean = jnp.sum(hist * ylog, axis=1, keepdims=True) / weight_sum
    xdev = centers[None, :] - xmean
    ydev = ylog - ymean
    sxx = jnp.maximum(jnp.sum(hist * xdev * xdev, axis=1) / weight_sum[:, 0], 0.05)
    syy = jnp.maximum(jnp.sum(hist * ydev * ydev, axis=1) / weight_sum[:, 0], 0.05)
    sxy = jnp.sum(hist * xdev * ydev, axis=1) / weight_sum[:, 0]
    return (-sxy * jnp.abs(sxy) / (sxx * syy), sxy / sxx)


def on_device(expression, power_order):
    samples = expression.shape[1]
    powers = power_order.shape[0]
    bins = 128
    genes_total = expression.shape[0] * lax.axis_size(ROW) * lax.axis_size(COL)
    panel = gather_directly(expression, COL, 0)
    partial_value = power_sums(
        panel, lax.all_gather(expression, ROW, axis=0, tiled=True), samples, powers
    )
    conn = sum_at_owner(partial_value, COL, 0)
    selector = (power_order[:, None] == jnp.arange(powers, dtype=jnp.int32)[None, :]).astype(
        jnp.float32
    )
    picked = jnp.dot(conn, selector.T, precision=lax.Precision.HIGHEST)
    log_conn = jnp.log(picked)
    log_total = math.log(genes_total)
    position = log_conn * ((bins - 1) / log_total)
    levels = jnp.arange(bins, dtype=jnp.float32)
    weights = jnp.maximum(0.0, 1.0 - jnp.abs(position[:, :, None] - levels[None, None, :]))
    local_hist = jnp.sum(weights, axis=0)
    hist = over_axes(local_hist, ROW_COL)
    fit, slope = scale_free_fit(hist, log_total, bins)
    return (log_conn, fit, slope)


def solution(mesh):
    torus = Mesh(mesh.devices.reshape(8, 4, 4, 2), ("row_0", "row_1", "col_0", "col_1"))
    return jax.shard_map(
        on_device,
        mesh=torus,
        in_specs=(P(ROW_COL, None), P()),
        out_specs=(P(ROW_COL, None), P(), P()),
        check_vma=False,
    )
```

profile of v0, /device:TPU:1, one launch (start us, length us, event | category | flops | bytes accessed | tf_op | source)
XLA Modules:
  0.0 238.8 jit_solution(6960383103107341380)
XLA Ops:
  7.2 0.0 all-gather.2.cloned.1.call-start
  7.2 0.7 all-gather.2.cloned.1.call-update
  7.9 1.2 broadcast_in_dim.2
  9.1 31.9 %all_to_all.10 = bf16[8,128,1024]{2,1,0:T(8,128)(2,1)S(1)} all-to-all(bf16[8,128,1024]{2,1,0:T(8,128)(2,1)S(1)} %broadcast_in_dim.2), channel_id=1, replica_groups=mesh['row_0'=8,'row_1'=4,'col_0'=4,'col_1'=2] {'col_0','col_1'}, dimensions={0} | all-to-all | bytes 4194304 | tf_op jit(solution)/shard_map/all_to_all | solution.py:17
  41.0 70.6 %all-gather.2.cloned.1.call-done = bf16[4096,1024]{1,0:T(8,128)(2,1)} async-done(((bf16[128,1024]{1,0:T(8,128)(2,1)}), bf16[4096,1024]{1,0:T(8,128)(2,1)}) %all-gather.2.cloned.1.call-update) | async-done | bytes 8388624 | tf_op jit(solution)/shard_map/all_gather | solution.py:84
  111.5 0.0 copy-start
  111.5 43.9 %multiply_reduce_fusion = (f32[1024]{0:T(1024)S(1)}, f32[1024]{0:T(1024)S(1)}, f32[1024]{0:T(1024)S(1)}, f32[1024]{0:T(1024)S(1)}, f32[1024]{0:T(1024)S(1)}, /*i...) fusion(bf16[1024,1024]{1,0:T(8,128)(2,1)S(1)} %bitcast.44, ...), kind=kOutput, calls=%fused_computation | convolution fusion | flops 8761880576 | bytes 10567680 | tf_op jit(solution)/shard_map/dot_general | solution.py:49
  155.6 0.6 copy.10
  156.3 5.7 %all-to-all-start.1 = ((f32[8,128,20]{1,2,0:T(8,128)}), f32[8,128,20]{1,2,0:T(8,128)S(1)}, u32[]{:S(2)}, u32[]{:S(2)}) async-start(f32[8,128,20]{1,2,0:T(8,128)} %copy.10), calls=%async_computation.1 | async-start | bytes 196608 | tf_op jit(solution)/shard_map/all_to_all | solution.py:39
  161.9 5.0 %all-to-all-done.1 = f32[8,128,20]{1,2,0:T(8,128)S(1)} async-done(((f32[8,128,20]{1,2,0:T(8,128)}), f32[8,128,20]{1,2,0:T(8,128)S(1)}, u32[]{:S(2)}, u32[]{:S(2)}) %all-to-all-start.1) | async-done | bytes 81952 | tf_op jit(solution)/shard_map/all_to_all | solution.py:39
  166.9 0.0 copy-done
  166.9 0.8 broadcast_multiply_fusion
  167.7 0.4 maximum_reduce_fusion
  168.2 21.0 %psum.28 = f32[20,128]{1,0:T(8,128)S(1)} all-reduce(f32[20,128]{1,0:T(8,128)S(1)} %maximum_reduce_fusion), channel_id=1, replica_groups=mesh['row_0'=8,'row_1'=4,'col_0'=4,'col_1'=2] {'row_0'}, use_global_device_ids=true, to_apply=%region_22.0 | all-reduce | flops 2560 | bytes 20480 | tf_op jit(solution)/shard_map/psum | solution.py:44
  189.2 11.2 %psum.29 = f32[20,128]{1,0:T(8,128)S(1)} all-reduce(f32[20,128]{1,0:T(8,128)S(1)} %psum.28), channel_id=1, replica_groups=mesh['row_0'=8,'row_1'=4,'col_0'=4,'col_1'=2] {'row_1'}, use_global_device_ids=true, to_apply=%region_23.0 | all-reduce | flops 2560 | bytes 20480 | tf_op jit(solution)/shard_map/psum | solution.py:44
  200.3 11.6 %psum.30 = f32[20,128]{1,0:T(8,128)S(1)} all-reduce(f32[20,128]{1,0:T(8,128)S(1)} %psum.29), channel_id=1, replica_groups=mesh['row_0'=8,'row_1'=4,'col_0'=4,'col_1'=2] {'col_0'}, use_global_device_ids=true, to_apply=%region_24.0 | all-reduce | flops 2560 | bytes 20480 | tf_op jit(solution)/shard_map/psum | solution.py:44
  211.9 18.6 %psum.31 = f32[20,128]{1,0:T(8,128)S(1)} all-reduce(f32[20,128]{1,0:T(8,128)S(1)} %psum.30), channel_id=1, replica_groups=mesh['row_0'=8,'row_1'=4,'col_0'=4,'col_1'=2] {'col_1'}, use_global_device_ids=true, to_apply=%region_25.0 | all-reduce | flops 2560 | bytes 20480 | tf_op jit(solution)/shard_map/psum | solution.py:44
  230.5 0.2 multiply_reduce_fusion.11
  230.7 0.2 multiply_reduce_fusion.10
  230.9 0.5 multiply_divide_fusion
  231.4 0.5 multiply_divide_fusion.1
  (23 shorter events, 0.1 us)
Async XLA Ops:
  7.2 104.4 %all-gather.2.cloned.1.call-start = ((), (), s32[]{:S(2)}) async-start(), calls=%async_computation.2 | async-start | bytes 8650752 | tf_op jit(solution)/shard_map/all_gather | solution.py:84
  111.5 55.4 %copy-start = (s32[20]{0:T(128)S(1)}, s32[20]{0:T(128)}, u32[]{:S(2)}) copy-start(s32[20]{0:T(128)} %param.3) | copy-start | bytes 244
  156.3 10.6 %all-to-all-start.1 = ((f32[8,128,20]{1,2,0:T(8,128)}), f32[8,128,20]{1,2,0:T(8,128)S(1)}, u32[]{:S(2)}, u32[]{:S(2)}) async-start(f32[8,128,20]{1,2,0:T(8,128)} %copy.10), calls=%async_computation.1 | async-start | bytes 196608 | tf_op jit(solution)/shard_map/all_to_all | solution.py:39
Sparse Core Ops, SparseCore 0:
  10.6 100.9 all-gather.1
where the time goes:
time: 239 us
  blocking collectives  94.2 us (39%)
  waiting for transfers between devices  76.2 us (32%)
  matrix products  44.7 us (19%)
  between operations  14.2 us (6%)
  starting transfers between devices  5.69 us (2%)
    all_gather x1, waiting for transfers between devices, on_device(): lax.all_gather(expression, ROW, axis=0, tiled=True)  70.6 us
    psum x4, blocking collectives, over_axes(): return functools.reduce(lax.psum, axes, x)  62.3 us
    dot_general x1, matrix products, power_sums(): lax.dot_general(rows, partners, (((1,), (1,)), ((), ())), preferred_eleme...  43.9 us
    all_to_all x1, blocking collectives, from_everyone(): return lax.all_to_all(copies, axis, split_axis=0, concat_axis=0, tiled=True)  31.9 us
    all_to_all x1, starting transfers between devices, sum_at_owner(): lax.all_to_all(tiles, axis, split_axis=0, concat_axis=0, tiled=True)  5.66 us
    all_to_all x1, waiting for transfers between devices, sum_at_owner(): lax.all_to_all(tiles, axis, split_axis=0, concat_axis=0, tiled=True)  4.97 us
  transfers between devices with their start and end apart: 2, of which 2 were waited for; matrix products, arithmetic and copies ran while one was open for 1% of the time, Pallas kernels for 0%

commit v1 on v0

v1 whole, which is shorter than its diff:
```python
import functools
import math

import jax
import jax.numpy as jnp
from jax import lax
from jax.experimental import pallas as pl
from jax.experimental.pallas import tpu as pltpu
from jax.sharding import Mesh
from jax.sharding import PartitionSpec as P

AXES = ("row_0", "row_1", "col_0", "col_1")
POWERS = 20
BINS = 128
LANES = 128
SLABS = 8
PIECE = 64
CHUNK = 256
STEPS = 8
MESH_ID = pl.DeviceIdType.MESH


def wrap4(d):
    return {0: 0, 1: 1, 2: 2, 3: -1}[d % 4]


X_UP = [(1, 0, 0), (1, 0, 1), (2, 0, 0), (1, 1, 1), (1, -1, 1), (2, 0, 1), (1, 2, 1)]
X_DOWN = [(-1, 0, 0), (-1, 0, 1), (-1, 1, 1), (-1, -1, 1), (-1, 2, 1), (2, 1, 1), (2, -1, 1), (2, 2, 1)]


def mirrored(order):
    return [(dy, dx, 1 - half) for dx, dy, half in order]


ARRIVALS = {
    (1, 0): X_UP,
    (-1, 0): X_DOWN,
    (0, 1): mirrored(X_UP),
    (0, -1): mirrored(X_DOWN),
}
LINKS = list(ARRIVALS)


def place_pieces():
    row, step_of = {}, {(0, 0, 0): 0, (0, 0, 1): 0}
    for step in range(1, STEPS + 1):
        free = {0: [0, 2], 1: [1, 3]}
        here = [order[step - 1] for order in ARRIVALS.values() if step <= len(order)]
        if step == STEPS:
            here = [(0, 0, 0), (0, 0, 1)] + here
        for piece in here:
            slot = free[piece[2]].pop(0)
            row[piece] = (step - 1) * CHUNK + slot * PIECE
            step_of.setdefault(piece, step)
    return row, step_of


ROW, STEP_OF = place_pieces()


def sends_by_step():
    out = [[] for _ in range(STEPS + 1)]
    for k, (lx, ly) in enumerate(LINKS):
        for i, (dx, dy, half) in enumerate(ARRIVALS[(lx, ly)]):
            mine = (wrap4(dx - lx), wrap4(dy - ly), half)
            out[STEP_OF[mine]].append((k, i, ROW[mine], ROW[(dx, dy, half)]))
    return out


PLANE_SENDS = sends_by_step()
PEERS = [(dx, dy) for dx in (0, 1, -1, 2) for dy in (0, 1, -1, 2) if (dx, dy) != (0, 0)]
Z_STEPS = 7
B_BLOCKS = [(0, 768), (768, 512), (1280, 512), (1792, 256)]


def tree_sum(values):
    while len(values) > 1:
        pairs = [a + b for a, b in zip(values[::2], values[1::2])]
        values = pairs + ([values[-1]] if len(values) % 2 else [])
    return values[0]


def kernel(
    log_total,
    samples,
    x_ref,
    order_ref,
    log_conn_ref,
    fit_ref,
    slope_ref,
    genes,
    partners,
    acc,
    tile,
    self_ref,
    outgoing,
    incoming,
    conn_ref,
    hist_ref,
    plane_ref,
    plane_hist,
    line_hist,
    local_sem,
    plane_send,
    plane_recv,
    z_send,
    z_recv,
    core_send,
    core_recv,
    part_send,
    part_recv,
    hist_send,
    hist_recv,
    line_send,
    line_recv,
):
    z, y, x, core = (lax.axis_index(a) for a in AXES)

    def at(dx=0, dy=0, dz=0, dc=0):
        return (
            lax.rem(z + (dz + 8), 8),
            lax.rem(y + (dy + 4), 4),
            lax.rem(x + (dx + 4), 4),
            lax.rem(core + dc, 2),
        )

    own_row = ROW[(0, 0, 0)]
    loads = []
    for k in range(SLABS):
        cols = pl.ds(k * LANES, LANES)
        loads.append(
            pltpu.make_async_copy(
                x_ref.at[:, cols], genes.at[k, pl.ds(own_row, 2 * PIECE), :], local_sem.at[0, k]
            )
        )
        loads.append(
            pltpu.make_async_copy(
                x_ref.at[:, cols], partners.at[k, pl.ds(0, 2 * PIECE), :], local_sem.at[1, k]
            )
        )
    for copy in loads:
        copy.start()

    barrier = pltpu.get_barrier_semaphore()
    near = [at(dx=1), at(dx=-1), at(dy=1), at(dy=-1), at(dz=1), at(dz=-1), at(dc=1)]
    for device in near:
        pl.semaphore_signal(barrier, inc=1, device_id=device, device_id_type=MESH_ID)
    acc[...] = jnp.zeros_like(acc)
    for copy in loads:
        copy.wait()
    pl.semaphore_wait(barrier, len(near))

    sent = []

    def remote(src, dst, send_sem, recv_sem, device):
        return pltpu.make_async_remote_copy(
            src_ref=src,
            dst_ref=dst,
            send_sem=send_sem,
            recv_sem=recv_sem,
            device_id=device,
            device_id_type=MESH_ID,
        )

    def plane_copy(k, i, src, dst):
        lx, ly = LINKS[k]
        return remote(
            genes.at[:, pl.ds(src, PIECE), :],
            genes.at[:, pl.ds(dst, PIECE), :],
            plane_send.at[k, i],
            plane_recv.at[k, i],
            at(dx=-lx, dy=-ly),
        )

    def z_row(direction, step):
        return step * CHUNK + (0 if direction == 1 else PIECE)

    def z_copy(direction, step):
        if step <= 2:
            first = step == 1
            src = 0 if first == (direction == 1) else PIECE
        else:
            src = z_row(direction, step - 2)
        side = 0 if direction == 1 else 1
        return remote(
            partners.at[:, pl.ds(src, PIECE), :],
            partners.at[:, pl.ds(z_row(direction, step), PIECE), :],
            z_send.at[side, step - 1],
            z_recv.at[side, step - 1],
            at(dz=-direction),
        )

    def core_copy(step):
        return remote(
            partners.at[:, pl.ds(step * CHUNK, 2 * PIECE), :],
            partners.at[:, pl.ds(step * CHUNK + 2 * PIECE, 2 * PIECE), :],
            core_send.at[step],
            core_recv.at[step],
            at(dc=1),
        )

    def start(copy):
        copy.start()
        sent.append(copy)

    def communicate(step):
        if step:
            for k, link in enumerate(LINKS):
                if step <= len(ARRIVALS[link]):
                    plane_copy(k, step - 1, 0, ROW[ARRIVALS[link][step - 1]]).wait_recv()
            if step <= Z_STEPS:
                for direction in (1, -1):
                    z_copy(direction, step).wait_recv()
        for send in PLANE_SENDS[step]:
            start(plane_copy(*send))
        for later in (1, 2) if step == 0 else (step + 2,):
            if later <= Z_STEPS:
                for direction in (1, -1):
                    start(z_copy(direction, later))
        if step <= Z_STEPS:
            start(core_copy(step))

    def partner_rows_ready(step):
        core_copy(step).wait_recv()

    def lanes_of(ref, first, count):
        return jnp.concatenate(
            [ref[k, pl.ds(pl.multiple_of(first, PIECE), count), :] for k in range(SLABS)], axis=1
        )

    scale = 1.0 / samples

    def work(chunk, first, rows):
        base = pl.multiple_of(chunk * CHUNK, CHUNK)
        tile[pl.ds(0, rows), :] = lax.dot_general(
            lanes_of(partners, first, rows),
            lanes_of(genes, base, CHUNK),
            (((1,), (1,)), ((), ())),
            preferred_element_type=jnp.float32,
        )
        if first == 0:

            @pl.when(chunk == STEPS - 1)
            def _():
                block = tile[pl.ds(0, 2 * PIECE), pl.ds(0, 2 * PIECE)]
                same = lax.broadcasted_iota(jnp.int32, block.shape, 0) == lax.broadcasted_iota(
                    jnp.int32, block.shape, 1
                )
                own = jnp.sum(jnp.where(same, block, 0.0), axis=0, keepdims=True)
                self_ref[...] = jnp.abs(own) * scale
                tile[pl.ds(0, 2 * PIECE), pl.ds(0, 2 * PIECE)] = jnp.where(same, 0.0, block)

        for i in range(rows // 256):
            for j in range(CHUNK // LANES):
                magnitude = [
                    jnp.abs(
                        tile[pl.ds(i * 256 + q * 16, 16), pl.ds(j * LANES, LANES)].astype(
                            jnp.bfloat16
                        )
                        * scale
                    )
                    for q in range(16)
                ]
                current = magnitude
                for power in range(POWERS):
                    total = tree_sum(current).astype(jnp.float32)
                    acc[power, :, pl.ds(base + j * LANES, LANES)] += total[0:8] + total[8:16]
                    if power < POWERS - 1:
                        current = [a * b for a, b in zip(current, magnitude)]

    def work_over(chunks, block):
        first, rows = B_BLOCKS[block]

        def body(chunk, carry):
            work(chunk, first, rows)
            return carry

        lax.fori_loop(chunks[0], chunks[1], body, 0)

    communicate(0)
    for phase in range(4):
        for step in (2 * phase + 1, 2 * phase + 2):
            communicate(step)
        for step in [0, 1, 2] if phase == 0 else [2 * phase + 1, 2 * phase + 2]:
            if step <= Z_STEPS:
                partner_rows_ready(step)
        for block in range(phase):
            work_over((2 * phase, 2 * phase + 2), block)
        work_over((0, 2 * phase + 2), phase)

    sums = jnp.sum(acc[...], axis=1)
    low_half = lax.broadcasted_iota(jnp.int32, (POWERS, LANES), 1) < PIECE

    def sums_of(dx, dy):
        low, high = (ROW[(dx, dy, half)] // LANES * LANES for half in (0, 1))
        return jnp.where(low_half, sums[:, low : low + LANES], sums[:, high : high + LANES])

    for n, (dx, dy) in enumerate(PEERS):
        outgoing[n, pl.ds(0, POWERS), :] = sums_of(dx, dy)
        outgoing[n, pl.ds(POWERS, 4), :] = jnp.zeros((4, LANES), jnp.float32)

    def part_copy(n):
        dx, dy = PEERS[n]
        return remote(
            outgoing.at[n], incoming.at[n], part_send.at[n], part_recv.at[n], at(dx=dx, dy=dy)
        )

    for n in range(len(PEERS)):
        start(part_copy(n))
    total = sums_of(0, 0)
    own = self_ref[...]
    powers = [own]
    for _ in range(POWERS - 1):
        powers.append(powers[-1] * own)
    total = total + jnp.concatenate(powers, axis=0)
    for n in range(len(PEERS)):
        part_copy(n).wait_recv()
        total = total + incoming[n, pl.ds(0, POWERS), :]
    conn_ref[pl.ds(0, POWERS), :] = total
    picked = jnp.concatenate([conn_ref[pl.ds(order_ref[t], 1), :] for t in range(POWERS)], axis=0)
    log_conn = jnp.log(picked)
    log_conn_ref[...] = log_conn

    position = log_conn * ((BINS - 1) / log_total)
    position = jnp.concatenate(
        [position, jnp.zeros((LANES - POWERS, LANES), jnp.float32)], axis=0
    ).T
    levels = lax.broadcasted_iota(jnp.int32, (LANES, BINS), 1).astype(jnp.float32)
    for t in range(POWERS):
        weights = jnp.maximum(0.0, 1.0 - jnp.abs(position[:, t : t + 1] - levels))
        hist_ref[pl.ds(t, 1), :] = jnp.sum(weights, axis=0, keepdims=True)
    hist_ref[pl.ds(POWERS, 4), :] = jnp.zeros((4, BINS), jnp.float32)

    here = x * 4 + y

    def hist_copy(n, src):
        dx, dy = PEERS[n]
        return remote(
            hist_ref, plane_hist.at[src], hist_send.at[n], hist_recv.at[n], at(dx=dx, dy=dy)
        )

    for n in range(len(PEERS)):
        start(hist_copy(n, here))
    plane_hist[here] = hist_ref[...]
    for n in range(len(PEERS)):
        dx, dy = PEERS[n]
        hist_copy(n, lax.rem(x + (4 - dx), 4) * 4 + lax.rem(y + (4 - dy), 4)).wait_recv()
    plane_ref[...] = tree_sum([plane_hist[i] for i in range(16)])

    line = z * 2 + core
    line_peers = [(dz, dc) for dz in range(8) for dc in range(2) if (dz, dc) != (0, 0)]

    def line_copy(n, src):
        dz, dc = line_peers[n]
        return remote(
            plane_ref, line_hist.at[src], line_send.at[n], line_recv.at[n], at(dz=dz, dc=dc)
        )

    for n in range(len(line_peers)):
        start(line_copy(n, line))
    line_hist[line] = plane_ref[...]
    for n in range(len(line_peers)):
        dz, dc = line_peers[n]
        line_copy(n, lax.rem(z + (8 - dz), 8) * 2 + lax.rem(core + dc, 2)).wait_recv()
    hist = tree_sum([line_hist[i] for i in range(16)])

    hist = jnp.concatenate([hist, jnp.zeros((LANES - 24, BINS), jnp.float32)], axis=0).T
    centers = lax.broadcasted_iota(jnp.int32, hist.shape, 0).astype(jnp.float32) * (
        log_total / (BINS - 1)
    )

    def over_bins(value):
        return jnp.sum(value, axis=0, keepdims=True)

    weight_sum = over_bins(hist)
    ylog = jnp.log(hist + 1.0) - log_total
    xdev = centers - over_bins(hist * centers) / weight_sum
    ydev = ylog - over_bins(hist * ylog) / weight_sum
    sxx = jnp.maximum(over_bins(hist * xdev * xdev) / weight_sum, 0.05)
    syy = jnp.maximum(over_bins(hist * ydev * ydev) / weight_sum, 0.05)
    sxy = over_bins(hist * xdev * ydev) / weight_sum
    fit_ref[...] = (-sxy * jnp.abs(sxy) / (sxx * syy))[:, :POWERS]
    slope_ref[...] = (sxy / sxx)[:, :POWERS]

    for copy in sent:
        copy.wait_send()


def on_device(expression, power_order):
    genes_dev, samples = expression.shape
    powers = power_order.shape[0]
    total_genes = genes_dev * lax.axis_size(AXES)
    plane, line = len(PEERS), 15
    dma = pltpu.SemaphoreType.DMA
    log_conn, fit, slope = pl.pallas_call(
        functools.partial(kernel, math.log(total_genes), samples),
        out_shape=(
            jax.ShapeDtypeStruct((powers, genes_dev), jnp.float32),
            jax.ShapeDtypeStruct((1, powers), jnp.float32),
            jax.ShapeDtypeStruct((1, powers), jnp.float32),
        ),
        in_specs=[pl.BlockSpec(memory_space=pl.ANY), pl.BlockSpec(memory_space=pltpu.SMEM)],
        out_specs=(pl.BlockSpec(memory_space=pltpu.VMEM),) * 3,
        scratch_shapes=[
            pltpu.VMEM((SLABS, 2048, LANES), jnp.bfloat16),
            pltpu.VMEM((SLABS, 2048, LANES), jnp.bfloat16),
            pltpu.VMEM((POWERS, 8, 2048), jnp.float32),
            pltpu.VMEM((768, CHUNK), jnp.float32),
            pltpu.VMEM((1, LANES), jnp.float32),
            pltpu.VMEM((plane, 24, LANES), jnp.float32),
            pltpu.VMEM((plane, 24, LANES), jnp.float32),
            pltpu.VMEM((24, LANES), jnp.float32),
            pltpu.VMEM((24, BINS), jnp.float32),
            pltpu.VMEM((24, BINS), jnp.float32),
            pltpu.VMEM((16, 24, BINS), jnp.float32),
            pltpu.VMEM((16, 24, BINS), jnp.float32),
            dma((2, SLABS)),
            dma((4, STEPS)),
            dma((4, STEPS)),
            dma((2, Z_STEPS)),
            dma((2, Z_STEPS)),
            dma((STEPS,)),
            dma((STEPS,)),
            dma((plane,)),
            dma((plane,)),
            dma((plane,)),
            dma((plane,)),
            dma((line,)),
            dma((line,)),
        ],
        compiler_params=pltpu.CompilerParams(
            collective_id=0, has_side_effects=True, vmem_limit_bytes=48 * 1024 * 1024
        ),
        name="coexpression",
    )(expression, power_order)
    return log_conn.T, fit.reshape(powers), slope.reshape(powers)


def solution(mesh):
    torus = Mesh(mesh.devices.reshape(8, 4, 4, 2), AXES)
    along = P(AXES, None)
    return jax.shard_map(
        on_device,
        mesh=torus,
        in_specs=(along, P()),
        out_specs=(along, P(), P()),
        check_vma=False,
    )
```

time: 239 us -> 78 us (0.33)
  blocking collectives: 94.2 us -> 0 us
  waiting for transfers between devices: 76.2 us -> 0 us
  Pallas kernels: 0 us -> 74 us
  matrix products: 44.7 us -> 0 us
  between operations: 14.2 us -> 0.65 us
  starting transfers between devices: 5.69 us -> 0 us
    pallas_call x0 -> x1, Pallas kernels: none -> 74 us  [on_device(): pl.pallas_call(functools.partial(kernel, math.log(total_genes), samples),...]
    all_gather x1 -> x0, waiting for transfers between devices: 70.6 us -> none  [on_device(): lax.all_gather(expression, ROW, axis=0, tiled=True)]
    psum x4 -> x0, blocking collectives: 62.3 us -> none  [over_axes(): return functools.reduce(lax.psum, axes, x)]
    dot_general x2 -> x0, matrix products: 44.7 us -> none  [the longest x1 43.9 us: power_sums(): lax.dot_general(rows, partners, (((1,), (1,)), ((), ())), preferred_eleme...]
    all_to_all x1 -> x0, blocking collectives: 31.9 us -> none  [from_everyone(): return lax.all_to_all(copies, axis, split_axis=0, concat_axis=0, tiled=True)]
    all_to_all x1 -> x0, starting transfers between devices: 5.66 us -> none  [sum_at_owner(): lax.all_to_all(tiles, axis, split_axis=0, concat_axis=0, tiled=True)]
    all_to_all x1 -> x0, waiting for transfers between devices: 4.97 us -> none  [sum_at_owner(): lax.all_to_all(tiles, axis, split_axis=0, concat_axis=0, tiled=True)]
    unnamed x21 -> x7, local copies, waits for them, and re-layouts: 0.06 us -> 3.22 us
  transfers between devices with their start and end apart: 2 -> 0, of which waited for: 2 -> 0; matrix products, arithmetic and copies ran while one was open for 1% -> 0% of each run, Pallas kernels for 0% -> 0%
where the time goes in v1:
time: 78 us; the launch traced here: 77.9 us
  Pallas kernels  74 us (95%)
  local copies, waits for them, and re-layouts  3.22 us (4%)
    pallas_call x1, Pallas kernels, on_device(): pl.pallas_call(functools.partial(kernel, math.log(total_genes), samples),...  74 us
    unnamed x7, local copies, waits for them, and re-layouts  3.22 us

profile of v1, /device:TPU:1, one launch (start us, length us, event | category | flops | bytes accessed | tf_op | source)
XLA Modules:
  0.0 77.9 jit_solution(11222743076598259973)
XLA Ops:
  0.6 0.0 copy-start
  0.6 0.9 %copy-done = bf16[128,1024]{1,0:T(8,128)(2,1)S(1)} copy-done((bf16[128,1024]{1,0:T(8,128)(2,1)S(1)}, bf16[128,1024]{1,0:T(8,128)(2,1)}, u32[]{:S(2)}) %copy-start) | copy-done | bytes 262168
  1.6 0.0 copy-start.1
  1.6 0.7 copy-done.1
  2.2 74.0 %coexpression.1 = (f32[20,128]{1,0:T(8,128)S(1)}, f32[1,20]{1,0:T(1,128)S(1)}, f32[1,20]{1,0:T(1,128)S(1)}) custom-call(bf16[128,1024]{1,0:T(8,128)(2,1)S(1)} %copy-done, s32[20]{0:T(128)S(1)} %copy-done.1), custom_call_target="tpu_custom_call" | custom-call | tf_op jit(solution)/shard_map/coexpression/pallas_call | solution.py:395
  76.3 0.6 copy.8
  76.9 0.5 copy.9
  77.4 0.5 copy.10
Async XLA Ops:
  0.6 1.0 %copy-start = (bf16[128,1024]{1,0:T(8,128)(2,1)S(1)}, bf16[128,1024]{1,0:T(8,128)(2,1)}, u32[]{:S(2)}) copy-start(bf16[128,1024]{1,0:T(8,128)(2,1)} %x_ref.1) | copy-start | bytes 786436
  1.6 0.7 copy-start.1

commit v2 on v1

--- a/solution.py
+++ b/solution.py
@@ -17,6 +17,7 @@
 PIECE = 64
 CHUNK = 256
 STEPS = 8
+TOKEN_POWER = 16
 MESH_ID = pl.DeviceIdType.MESH
 
 
@@ -70,7 +71,42 @@
 PLANE_SENDS = sends_by_step()
 PEERS = [(dx, dy) for dx in (0, 1, -1, 2) for dy in (0, 1, -1, 2) if (dx, dy) != (0, 0)]
 Z_STEPS = 7
-B_BLOCKS = [(0, 768), (768, 512), (1280, 512), (1792, 256)]
+ROWS = 512
+ITEMS = (
+    [(0, 0), (1, 0), (2, 0), (0, 1), (1, 1), (2, 1), (3, 0), (3, 1), (4, 0), (4, 1)]
+    + [(c, 2) for c in range(5)]
+    + [(5, 0), (5, 1), (5, 2), (6, 0), (6, 1), (6, 2), (7, 0), (7, 1), (7, 2)]
+    + [(7 - c, 3) for c in range(8)]
+)
+BEFORE = {
+    0: ([1, 2], [0, 1]),
+    2: ([3], [2, 3]),
+    6: ([4], []),
+    8: ([5], []),
+    10: ([], [4, 5]),
+    14: ([6], []),
+    18: ([7], []),
+    20: ([8], []),
+    24: ([], [6, 7]),
+}
+OWN_ITEM = ITEMS.index((STEPS - 1, 0))
+
+
+def item_at(n):
+    chunk, block = jnp.int32(0), jnp.int32(0)
+    for k, (c, b) in enumerate(ITEMS):
+        chunk = jnp.where(n == k, c, chunk)
+        block = jnp.where(n == k, b, block)
+    return chunk, block
+
+
+def peers_after(first_chunk, last_chunk):
+    out = []
+    for n, (dx, dy) in enumerate(PEERS):
+        lowest = min(ROW[(dx, dy, half)] // CHUNK for half in (0, 1))
+        if first_chunk <= lowest < last_chunk:
+            out.append(n)
+    return out
 
 
 def tree_sum(values):
@@ -91,7 +127,8 @@
     genes,
     partners,
     acc,
-    tile,
+    tile_even,
+    tile_odd,
     self_ref,
     outgoing,
     incoming,
@@ -100,6 +137,11 @@
     plane_ref,
     plane_hist,
     line_hist,
+    core_hist,
+    line_ref,
+    results,
+    fit_out,
+    slope_out,
     local_sem,
     plane_send,
     plane_recv,
@@ -113,6 +155,9 @@
     hist_recv,
     line_send,
     line_recv,
+    last_send,
+    last_recv,
+    out_sem,
 ):
     z, y, x, core = (lax.axis_index(a) for a in AXES)
 
@@ -149,8 +194,6 @@
     for copy in loads:
         copy.wait()
     pl.semaphore_wait(barrier, len(near))
-
-    sent = []
 
     def remote(src, dst, send_sem, recv_sem, device):
         return pltpu.make_async_remote_copy(
@@ -199,10 +242,6 @@
             at(dc=1),
         )
 
-    def start(copy):
-        copy.start()
-        sent.append(copy)
-
     def communicate(step):
         if step:
             for k, link in enumerate(LINKS):
@@ -212,13 +251,13 @@
                 for direction in (1, -1):
                     z_copy(direction, step).wait_recv()
         for send in PLANE_SENDS[step]:
-            start(plane_copy(*send))
+            plane_copy(*send).start()
         for later in (1, 2) if step == 0 else (step + 2,):
             if later <= Z_STEPS:
                 for direction in (1, -1):
-                    start(z_copy(direction, later))
+                    z_copy(direction, later).start()
         if step <= Z_STEPS:
-            start(core_copy(step))
+            core_copy(step).start()
 
     def partner_rows_ready(step):
         core_copy(step).wait_recv()
@@ -230,27 +269,19 @@
 
     scale = 1.0 / samples
 
-    def work(chunk, first, rows):
-        base = pl.multiple_of(chunk * CHUNK, CHUNK)
-        tile[pl.ds(0, rows), :] = lax.dot_general(
-            lanes_of(partners, first, rows),
-            lanes_of(genes, base, CHUNK),
+    def multiply(tile, item):
+        chunk, block = item
+        tile[pl.ds(0, ROWS), :] = lax.dot_general(
+            lanes_of(partners, block * ROWS, ROWS),
+            lanes_of(genes, chunk * CHUNK, CHUNK),
             (((1,), (1,)), ((), ())),
             preferred_element_type=jnp.float32,
         )
-        if first == 0:
-
-            @pl.when(chunk == STEPS - 1)
-            def _():
-                block = tile[pl.ds(0, 2 * PIECE), pl.ds(0, 2 * PIECE)]
-                same = lax.broadcasted_iota(jnp.int32, block.shape, 0) == lax.broadcasted_iota(
-                    jnp.int32, block.shape, 1
-                )
-                own = jnp.sum(jnp.where(same, block, 0.0), axis=0, keepdims=True)
-                self_ref[...] = jnp.abs(own) * scale
-                tile[pl.ds(0, 2 * PIECE), pl.ds(0, 2 * PIECE)] = jnp.where(same, 0.0, block)
-
-        for i in range(rows // 256):
+
+    def accumulate(tile, item):
+        base = pl.multiple_of(item[0] * CHUNK, CHUNK)
+        token = pl.multiple_of(ROWS + 8 * item[0], 8)
+        for i in range(ROWS // 256):
             for j in range(CHUNK // LANES):
                 magnitude = [
                     jnp.abs(
@@ -264,40 +295,29 @@
                 current = magnitude
                 for power in range(POWERS):
                     total = tree_sum(current).astype(jnp.float32)
-                    acc[power, :, pl.ds(base + j * LANES, LANES)] += total[0:8] + total[8:16]
+                    total = total[0:8] + total[8:16]
+                    acc[power, :, pl.ds(base + j * LANES, LANES)] += total
+                    if power == TOKEN_POWER:
+                        tile[pl.ds(token, 8), pl.ds(0, LANES)] = total
                     if power < POWERS - 1:
                         current = [a * b for a, b in zip(current, magnitude)]
 
-    def work_over(chunks, block):
-        first, rows = B_BLOCKS[block]
-
-        def body(chunk, carry):
-            work(chunk, first, rows)
-            return carry
-
-        lax.fori_loop(chunks[0], chunks[1], body, 0)
-
-    communicate(0)
-    for phase in range(4):
-        for step in (2 * phase + 1, 2 * phase + 2):
-            communicate(step)
-        for step in [0, 1, 2] if phase == 0 else [2 * phase + 1, 2 * phase + 2]:
-            if step <= Z_STEPS:
-                partner_rows_ready(step)
-        for block in range(phase):
-            work_over((2 * phase, 2 * phase + 2), block)
-        work_over((0, 2 * phase + 2), phase)
-
-    sums = jnp.sum(acc[...], axis=1)
-    low_half = lax.broadcasted_iota(jnp.int32, (POWERS, LANES), 1) < PIECE
+    def keep_self_apart(tile):
+        block = tile[pl.ds(0, 2 * PIECE), pl.ds(0, 2 * PIECE)]
+        same = lax.broadcasted_iota(jnp.int32, block.shape, 0) == lax.broadcasted_iota(
+            jnp.int32, block.shape, 1
+        )
+        own = jnp.sum(jnp.where(same, block, 0.0), axis=0, keepdims=True)
+        self_ref[...] = jnp.abs(own) * scale
+        tile[pl.ds(0, 2 * PIECE), pl.ds(0, 2 * PIECE)] = jnp.where(same, 0.0, block)
+
+    low_half = lax.broadcasted_iota(jnp.int32, (POWERS, 8, LANES), 2) < PIECE
 
     def sums_of(dx, dy):
-        low, high = (ROW[(dx, dy, half)] // LANES * LANES for half in (0, 1))
-        return jnp.where(low_half, sums[:, low : low + LANES], sums[:, high : high + LANES])
-
-    for n, (dx, dy) in enumerate(PEERS):
-        outgoing[n, pl.ds(0, POWERS), :] = sums_of(dx, dy)
-        outgoing[n, pl.ds(POWERS, 4), :] = jnp.zeros((4, LANES), jnp.float32)
+        low, high = (
+            acc[:, :, pl.ds(ROW[(dx, dy, half)] // LANES * LANES, LANES)] for half in (0, 1)
+        )
+        return jnp.sum(jnp.where(low_half, low, high), axis=1)
 
     def part_copy(n):
         dx, dy = PEERS[n]
@@ -305,8 +325,43 @@
             outgoing.at[n], incoming.at[n], part_send.at[n], part_recv.at[n], at(dx=dx, dy=dy)
         )
 
-    for n in range(len(PEERS)):
-        start(part_copy(n))
+    def send_parts(first_chunk, last_chunk):
+        for n in peers_after(first_chunk, last_chunk):
+            outgoing[n] = sums_of(*PEERS[n])
+            part_copy(n).start()
+
+    sends = {28: (5, 8), 30: (3, 5)}
+
+    def prepare(u):
+        for n in range(0, len(ITEMS), 2):
+            if n in BEFORE or n in sends or n == OWN_ITEM + 1:
+
+                @pl.when(u == n // 2)
+                def _():
+                    steps, rows = BEFORE.get(n, ([], []))
+                    for step in steps:
+                        communicate(step)
+                    for step in rows:
+                        partner_rows_ready(step)
+                    if n == OWN_ITEM + 1:
+                        keep_self_apart((tile_even, tile_odd)[OWN_ITEM % 2])
+                    if n in sends:
+                        send_parts(*sends[n])
+
+    communicate(0)
+    tile_odd[...] = jnp.zeros_like(tile_odd)
+
+    def body(u, carry):
+        prepare(u)
+        multiply(tile_even, item_at(2 * u))
+        accumulate(tile_odd, item_at(2 * u - 1))
+        multiply(tile_odd, item_at(2 * u + 1))
+        accumulate(tile_even, item_at(2 * u))
+        return carry
+
+    lax.fori_loop(0, len(ITEMS) // 2, body, 0)
+    accumulate(tile_odd, item_at(jnp.int32(len(ITEMS) - 1)))
+    send_parts(0, 3)
     total = sums_of(0, 0)
     own = self_ref[...]
     powers = [own]
@@ -315,11 +370,13 @@
     total = total + jnp.concatenate(powers, axis=0)
     for n in range(len(PEERS)):
         part_copy(n).wait_recv()
-        total = total + incoming[n, pl.ds(0, POWERS), :]
-    conn_ref[pl.ds(0, POWERS), :] = total
+        total = total + incoming[n]
+    conn_ref[...] = total
     picked = jnp.concatenate([conn_ref[pl.ds(order_ref[t], 1), :] for t in range(POWERS)], axis=0)
     log_conn = jnp.log(picked)
-    log_conn_ref[...] = log_conn
+    results[pl.ds(0, POWERS), :] = log_conn
+    out_copies = [pltpu.make_async_copy(results.at[pl.ds(0, POWERS), :], log_conn_ref, out_sem.at[0])]
+    out_copies[0].start()
 
     position = log_conn * ((BINS - 1) / log_total)
     position = jnp.concatenate(
@@ -329,7 +386,6 @@
     for t in range(POWERS):
         weights = jnp.maximum(0.0, 1.0 - jnp.abs(position[:, t : t + 1] - levels))
         hist_ref[pl.ds(t, 1), :] = jnp.sum(weights, axis=0, keepdims=True)
-    hist_ref[pl.ds(POWERS, 4), :] = jnp.zeros((4, BINS), jnp.float32)
 
     here = x * 4 + y
 
@@ -340,31 +396,30 @@
         )
 
     for n in range(len(PEERS)):
-        start(hist_copy(n, here))
+        hist_copy(n, here).start()
     plane_hist[here] = hist_ref[...]
     for n in range(len(PEERS)):
         dx, dy = PEERS[n]
         hist_copy(n, lax.rem(x + (4 - dx), 4) * 4 + lax.rem(y + (4 - dy), 4)).wait_recv()
     plane_ref[...] = tree_sum([plane_hist[i] for i in range(16)])
 
-    line = z * 2 + core
-    line_peers = [(dz, dc) for dz in range(8) for dc in range(2) if (dz, dc) != (0, 0)]
-
     def line_copy(n, src):
-        dz, dc = line_peers[n]
         return remote(
-            plane_ref, line_hist.at[src], line_send.at[n], line_recv.at[n], at(dz=dz, dc=dc)
-        )
-
-    for n in range(len(line_peers)):
-        start(line_copy(n, line))
-    line_hist[line] = plane_ref[...]
-    for n in range(len(line_peers)):
-        dz, dc = line_peers[n]
-        line_copy(n, lax.rem(z + (8 - dz), 8) * 2 + lax.rem(core + dc, 2)).wait_recv()
-    hist = tree_sum([line_hist[i] for i in range(16)])
-
-    hist = jnp.concatenate([hist, jnp.zeros((LANES - 24, BINS), jnp.float32)], axis=0).T
+            plane_ref, line_hist.at[src], line_send.at[n], line_recv.at[n], at(dz=n + 1)
+        )
+
+    for n in range(7):
+        line_copy(n, z).start()
+    line_hist[z] = plane_ref[...]
+    for n in range(7):
+        line_copy(n, lax.rem(z + (7 - n), 8)).wait_recv()
+    line_ref[...] = tree_sum([line_hist[i] for i in range(8)])
+    last = remote(line_ref, core_hist, last_send, last_recv, at(dc=1))
+    last.start()
+    last.wait_recv()
+    hist = line_ref[...] + core_hist[...]
+
+    hist = jnp.concatenate([hist, jnp.zeros((LANES - POWERS, BINS), jnp.float32)], axis=0).T
     centers = lax.broadcasted_iota(jnp.int32, hist.shape, 0).astype(jnp.float32) * (
         log_total / (BINS - 1)
     )
@@ -379,18 +434,35 @@
     sxx = jnp.maximum(over_bins(hist * xdev * xdev) / weight_sum, 0.05)
     syy = jnp.maximum(over_bins(hist * ydev * ydev) / weight_sum, 0.05)
     sxy = over_bins(hist * xdev * ydev) / weight_sum
-    fit_ref[...] = (-sxy * jnp.abs(sxy) / (sxx * syy))[:, :POWERS]
-    slope_ref[...] = (sxy / sxx)[:, :POWERS]
-
-    for copy in sent:
-        copy.wait_send()
+    fit_out[...] = (-sxy * jnp.abs(sxy) / (sxx * syy))[:, :POWERS]
+    slope_out[...] = (sxy / sxx)[:, :POWERS]
+    out_copies.append(pltpu.make_async_copy(fit_out, fit_ref, out_sem.at[1]))
+    out_copies.append(pltpu.make_async_copy(slope_out, slope_ref, out_sem.at[2]))
+    for copy in out_copies[1:]:
+        copy.start()
+    for sends in PLANE_SENDS:
+        for send in sends:
+            plane_copy(*send).wait_send()
+    for step in range(1, Z_STEPS + 1):
+        for direction in (1, -1):
+            z_copy(direction, step).wait_send()
+    for step in range(Z_STEPS + 1):
+        core_copy(step).wait_send()
+    for n in range(len(PEERS)):
+        part_copy(n).wait_send()
+        hist_copy(n, here).wait_send()
+    for n in range(7):
+        line_copy(n, z).wait_send()
+    last.wait_send()
+    for copy in out_copies:
+        copy.wait()
 
 
 def on_device(expression, power_order):
     genes_dev, samples = expression.shape
     powers = power_order.shape[0]
     total_genes = genes_dev * lax.axis_size(AXES)
-    plane, line = len(PEERS), 15
+    plane, line = len(PEERS), 7
     dma = pltpu.SemaphoreType.DMA
     log_conn, fit, slope = pl.pallas_call(
         functools.partial(kernel, math.log(total_genes), samples),
@@ -399,21 +471,27 @@
             jax.ShapeDtypeStruct((1, powers), jnp.float32),
             jax.ShapeDtypeStruct((1, powers), jnp.float32),
         ),
-        in_specs=[pl.BlockSpec(memory_space=pl.ANY), pl.BlockSpec(memory_space=pltpu.SMEM)],
-        out_specs=(pl.BlockSpec(memory_space=pltpu.VMEM),) * 3,
+        in_specs=[pl.BlockSpec(memory_space=pltpu.HBM), pl.BlockSpec(memory_space=pltpu.SMEM)],
+        out_specs=(pl.BlockSpec(memory_space=pltpu.HBM),) * 3,
         scratch_shapes=[
             pltpu.VMEM((SLABS, 2048, LANES), jnp.bfloat16),
             pltpu.VMEM((SLABS, 2048, LANES), jnp.bfloat16),
             pltpu.VMEM((POWERS, 8, 2048), jnp.float32),
-            pltpu.VMEM((768, CHUNK), jnp.float32),
+            pltpu.VMEM((ROWS + 8 * STEPS, CHUNK), jnp.float32),
+            pltpu.VMEM((ROWS + 8 * STEPS, CHUNK), jnp.float32),
             pltpu.VMEM((1, LANES), jnp.float32),
-            pltpu.VMEM((plane, 24, LANES), jnp.float32),
-            pltpu.VMEM((plane, 24, LANES), jnp.float32),
-            pltpu.VMEM((24, LANES), jnp.float32),
-            pltpu.VMEM((24, BINS), jnp.float32),
-            pltpu.VMEM((24, BINS), jnp.float32),
-            pltpu.VMEM((16, 24, BINS), jnp.float32),
-            pltpu.VMEM((16, 24, BINS), jnp.float32),
+            pltpu.VMEM((plane, powers, LANES), jnp.float32),
+            pltpu.VMEM((plane, powers, LANES), jnp.float32),
+            pltpu.VMEM((powers, LANES), jnp.float32),
+            pltpu.VMEM((powers, BINS), jnp.float32),
+            pltpu.VMEM((powers, BINS), jnp.float32),
+            pltpu.VMEM((16, powers, BINS), jnp.float32),
+            pltpu.VMEM((8, powers, BINS), jnp.float32),
+            pltpu.VMEM((powers, BINS), jnp.float32),
+            pltpu.VMEM((powers, BINS), jnp.float32),
+            pltpu.VMEM((powers, LANES), jnp.float32),
+            pltpu.VMEM((1, powers), jnp.float32),
+            pltpu.VMEM((1, powers), jnp.float32),
             dma((2, SLABS)),
             dma((4, STEPS)),
             dma((4, STEPS)),
@@ -427,9 +505,12 @@
             dma((plane,)),
             dma((line,)),
             dma((line,)),
+            dma,
+            dma,
+            dma((3,)),
         ],
         compiler_params=pltpu.CompilerParams(
-            collective_id=0, has_side_effects=True, vmem_limit_bytes=48 * 1024 * 1024
+            collective_id=0, has_side_effects=True, vmem_limit_bytes=67_043_328
         ),
         name="coexpression",
     )(expression, power_order)

time: 78 us -> 71.5 us (0.917)
  Pallas kernels: 74 us -> 68.2 us
  local copies, waits for them, and re-layouts: 3.22 us -> 2.43 us
    pallas_call x1, Pallas kernels: 74 us -> 68.2 us  [on_device(): pl.pallas_call(functools.partial(kernel, math.log(total_genes), samples),...]
    unnamed x7, local copies, waits for them, and re-layouts: 3.22 us -> 2.43 us
where the time goes in v2:
time: 71.5 us; the launch traced here: 71.2 us
  Pallas kernels  68.2 us (95%)
  local copies, waits for them, and re-layouts  2.43 us (3%)
    pallas_call x1, Pallas kernels, on_device(): pl.pallas_call(functools.partial(kernel, math.log(total_genes), samples),...  68.2 us
    unnamed x7, local copies, waits for them, and re-layouts  2.43 us

profile of v2, /device:TPU:1, one launch (start us, length us, event | category | flops | bytes accessed | tf_op | source)
XLA Modules:
  0.0 71.2 jit_solution(9281042312504930764)
XLA Ops:
  0.6 68.2 %coexpression.1 = (f32[20,128]{1,0:T(8,128)}, f32[1,20]{1,0:T(1,128)}, f32[1,20]{1,0:T(1,128)}) custom-call(bf16[128,1024]{1,0:T(8,128)(2,1)} %x_ref.1, s32[20]{0:T(128)} %order_ref.1), custom_call_target="tpu_custom_call" | custom-call | tf_op jit(solution)/shard_map/coexpression/pallas_call | solution.py:467
  68.8 0.0 copy-start.1
  68.8 1.3 %copy.8 = f32[128,20]{0,1:T(8,128)} copy(f32[128,20]{0,1:T(8,128)} %bitcast.3) | data formatting | bytes 20480
  70.1 0.0 copy-done.1
  70.1 0.0 copy-start
  70.1 0.5 copy.9
  70.6 0.1 copy-done
  70.7 0.5 copy.10
Async XLA Ops:
  68.8 1.3 %copy-start.1 = (f32[1,20]{1,0:T(1,128)S(1)}, f32[1,20]{1,0:T(1,128)}, u32[]{:S(2)}) copy-start(f32[1,20]{1,0:T(1,128)} %get-tuple-element.7) | copy-start | bytes 244
  70.1 0.6 copy-start

commit v3 on v2

--- a/solution.py
+++ b/solution.py
@@ -17,7 +17,7 @@
 PIECE = 64
 CHUNK = 256
 STEPS = 8
-TOKEN_POWER = 16
+SHARES = 4
 MESH_ID = pl.DeviceIdType.MESH
 
 
@@ -75,8 +75,8 @@
 ITEMS = (
     [(0, 0), (1, 0), (2, 0), (0, 1), (1, 1), (2, 1), (3, 0), (3, 1), (4, 0), (4, 1)]
     + [(c, 2) for c in range(5)]
-    + [(5, 0), (5, 1), (5, 2), (6, 0), (6, 1), (6, 2), (7, 0), (7, 1), (7, 2)]
-    + [(7 - c, 3) for c in range(8)]
+    + [(5, 0), (5, 1), (5, 2), (6, 0), (6, 1), (6, 2), (6, 3), (5, 3), (4, 3)]
+    + [(7, 1), (7, 0), (7, 2), (7, 3), (3, 3), (2, 3), (1, 3), (0, 3)]
 )
 BEFORE = {
     0: ([1, 2], [0, 1]),
@@ -86,8 +86,8 @@
     10: ([], [4, 5]),
     14: ([6], []),
     18: ([7], []),
-    20: ([8], []),
-    24: ([], [6, 7]),
+    20: ([], [6, 7]),
+    24: ([8], []),
 }
 OWN_ITEM = ITEMS.index((STEPS - 1, 0))
 
@@ -100,13 +100,17 @@
     return chunk, block
 
 
-def peers_after(first_chunk, last_chunk):
-    out = []
-    for n, (dx, dy) in enumerate(PEERS):
-        lowest = min(ROW[(dx, dy, half)] // CHUNK for half in (0, 1))
-        if first_chunk <= lowest < last_chunk:
-            out.append(n)
+def sends_before():
+    bounds = [28, 30, len(ITEMS) + 2]
+    out = {n: [] for n in bounds}
+    for peer, (dx, dy) in enumerate(PEERS):
+        chunks = [ROW[(dx, dy, half)] // CHUNK for half in (0, 1)]
+        done = max(n for n, (chunk, _) in enumerate(ITEMS) if chunk in chunks)
+        out[min(n for n in bounds if n - 2 >= done)].append(peer)
     return out
+
+
+PART_SENDS = sends_before()
 
 
 def tree_sum(values):
@@ -262,45 +266,52 @@
     def partner_rows_ready(step):
         core_copy(step).wait_recv()
 
-    def lanes_of(ref, first, count):
+    def lanes_of(ref, first, count, part):
+        slabs = range(part * SLABS // SHARES, (part + 1) * SLABS // SHARES)
         return jnp.concatenate(
-            [ref[k, pl.ds(pl.multiple_of(first, PIECE), count), :] for k in range(SLABS)], axis=1
+            [ref[k, pl.ds(pl.multiple_of(first, PIECE), count), :] for k in slabs], axis=1
         )
 
     scale = 1.0 / samples
 
-    def multiply(tile, item):
+    def multiply(tile, item, part):
         chunk, block = item
-        tile[pl.ds(0, ROWS), :] = lax.dot_general(
-            lanes_of(partners, block * ROWS, ROWS),
-            lanes_of(genes, chunk * CHUNK, CHUNK),
+        product = lax.dot_general(
+            lanes_of(partners, block * ROWS, ROWS, part),
+            lanes_of(genes, chunk * CHUNK, CHUNK, part),
             (((1,), (1,)), ((), ())),
             preferred_element_type=jnp.float32,
         )
-
-    def accumulate(tile, item):
+        if part == 0:
+            tile[pl.ds(0, ROWS), :] = product
+        else:
+            tile[pl.ds(0, ROWS), :] += product
+        return product[ROWS - 8 :, :LANES]
+
+    def accumulate(tile, item, unit):
         base = pl.multiple_of(item[0] * CHUNK, CHUNK)
-        token = pl.multiple_of(ROWS + 8 * item[0], 8)
-        for i in range(ROWS // 256):
-            for j in range(CHUNK // LANES):
-                magnitude = [
-                    jnp.abs(
-                        tile[pl.ds(i * 256 + q * 16, 16), pl.ds(j * LANES, LANES)].astype(
-                            jnp.bfloat16
-                        )
-                        * scale
-                    )
-                    for q in range(16)
-                ]
-                current = magnitude
-                for power in range(POWERS):
-                    total = tree_sum(current).astype(jnp.float32)
-                    total = total[0:8] + total[8:16]
-                    acc[power, :, pl.ds(base + j * LANES, LANES)] += total
-                    if power == TOKEN_POWER:
-                        tile[pl.ds(token, 8), pl.ds(0, LANES)] = total
-                    if power < POWERS - 1:
-                        current = [a * b for a, b in zip(current, magnitude)]
+        i, j = divmod(unit, CHUNK // LANES)
+        magnitude = [
+            jnp.abs(
+                tile[pl.ds(i * 256 + q * 16, 16), pl.ds(j * LANES, LANES)].astype(jnp.bfloat16)
+                * scale
+            )
+            for q in range(16)
+        ]
+        current = magnitude
+        for power in range(POWERS):
+            total = tree_sum(current).astype(jnp.float32)
+            acc[power, :, pl.ds(base + j * LANES, LANES)] += total[0:8] + total[8:16]
+            if power < POWERS - 1:
+                current = [a * b for a, b in zip(current, magnitude)]
+
+    def advance(tile, item, done_tile, done_item):
+        row = pl.multiple_of(ROWS + 8 * done_item[0], 8)
+        for share in range(SHARES):
+            last = multiply(tile, item, share)
+            accumulate(done_tile, done_item, share)
+            if share < SHARES - 1:
+                done_tile[pl.ds(row, 8), pl.ds(0, LANES)] = last
 
     def keep_self_apart(tile):
         block = tile[pl.ds(0, 2 * PIECE), pl.ds(0, 2 * PIECE)]
@@ -325,16 +336,14 @@
             outgoing.at[n], incoming.at[n], part_send.at[n], part_recv.at[n], at(dx=dx, dy=dy)
         )
 
-    def send_parts(first_chunk, last_chunk):
-        for n in peers_after(first_chunk, last_chunk):
+    def send_parts(before):
+        for n in PART_SENDS[before]:
             outgoing[n] = sums_of(*PEERS[n])
             part_copy(n).start()
 
-    sends = {28: (5, 8), 30: (3, 5)}
-
     def prepare(u):
         for n in range(0, len(ITEMS), 2):
-            if n in BEFORE or n in sends or n == OWN_ITEM + 1:
+            if n in BEFORE or n in PART_SENDS or n == OWN_ITEM + 1:
 
                 @pl.when(u == n // 2)
                 def _():
@@ -345,23 +354,25 @@
                         partner_rows_ready(step)
                     if n == OWN_ITEM + 1:
                         keep_self_apart((tile_even, tile_odd)[OWN_ITEM % 2])
-                    if n in sends:
-                        send_parts(*sends[n])
+                    if n in PART_SENDS:
+                        send_parts(n)
 
     communicate(0)
     tile_odd[...] = jnp.zeros_like(tile_odd)
 
     def body(u, carry):
+        before, first, second = carry
         prepare(u)
-        multiply(tile_even, item_at(2 * u))
-        accumulate(tile_odd, item_at(2 * u - 1))
-        multiply(tile_odd, item_at(2 * u + 1))
-        accumulate(tile_even, item_at(2 * u))
-        return carry
-
-    lax.fori_loop(0, len(ITEMS) // 2, body, 0)
-    accumulate(tile_odd, item_at(jnp.int32(len(ITEMS) - 1)))
-    send_parts(0, 3)
+        advance(tile_even, first, tile_odd, before)
+        advance(tile_odd, second, tile_even, first)
+        return second, item_at(2 * u + 2), item_at(2 * u + 3)
+
+    lax.fori_loop(
+        0, len(ITEMS) // 2, body, tuple(item_at(jnp.int32(n)) for n in (-1, 0, 1))
+    )
+    for unit in range(SHARES):
+        accumulate(tile_odd, item_at(jnp.int32(len(ITEMS) - 1)), unit)
+    send_parts(len(ITEMS) + 2)
     total = sums_of(0, 0)
     own = self_ref[...]
     powers = [own]
@@ -510,7 +521,7 @@
             dma((3,)),
         ],
         compiler_params=pltpu.CompilerParams(
-            collective_id=0, has_side_effects=True, vmem_limit_bytes=67_043_328
+            collective_id=0, has_side_effects=True, vmem_limit_bytes=66_800_000
         ),
         name="coexpression",
     )(expression, power_order)

time: 71.5 us -> 65.9 us (0.922)
  Pallas kernels: 68.2 us -> 62.6 us
    pallas_call x1, Pallas kernels: 68.2 us -> 62.6 us  [on_device(): pl.pallas_call(functools.partial(kernel, math.log(total_genes), samples),...]
where the time goes in v3:
time: 65.9 us; the launch traced here: 65.7 us
  Pallas kernels  62.6 us (95%)
  local copies, waits for them, and re-layouts  2.43 us (4%)
    pallas_call x1, Pallas kernels, on_device(): pl.pallas_call(functools.partial(kernel, math.log(total_genes), samples),...  62.6 us
    unnamed x7, local copies, waits for them, and re-layouts  2.43 us

profile of v3, /device:TPU:1, one launch (start us, length us, event | category | flops | bytes accessed | tf_op | source)
XLA Modules:
  0.0 65.7 jit_solution(3101450501567511363)
XLA Ops:
  0.6 62.6 %coexpression.1 = (f32[20,128]{1,0:T(8,128)}, f32[1,20]{1,0:T(1,128)}, f32[1,20]{1,0:T(1,128)}) custom-call(bf16[128,1024]{1,0:T(8,128)(2,1)} %x_ref.1, s32[20]{0:T(128)} %order_ref.1), custom_call_target="tpu_custom_call" | custom-call | tf_op jit(solution)/shard_map/coexpression/pallas_call | solution.py:478
  63.3 0.0 copy-start.1
  63.3 1.3 %copy.8 = f32[128,20]{0,1:T(8,128)} copy(f32[128,20]{0,1:T(8,128)} %bitcast.3) | data formatting | bytes 20480
  64.6 0.0 copy-done.1
  64.6 0.0 copy-start
  64.6 0.5 copy.9
  65.1 0.1 copy-done
  65.2 0.5 copy.10
Async XLA Ops:
  63.3 1.3 %copy-start.1 = (f32[1,20]{1,0:T(1,128)S(1)}, f32[1,20]{1,0:T(1,128)}, u32[]{:S(2)}) copy-start(f32[1,20]{1,0:T(1,128)} %get-tuple-element.7) | copy-start | bytes 244
  64.6 0.6 copy-start

commit v4 on v3

--- a/solution.py
+++ b/solution.py
@@ -69,7 +69,11 @@
 
 
 PLANE_SENDS = sends_by_step()
-PEERS = [(dx, dy) for dx in (0, 1, -1, 2) for dy in (0, 1, -1, 2) if (dx, dy) != (0, 0)]
+PEERS = sorted(
+    [(dx, dy) for dx in (0, 1, -1, 2) for dy in (0, 1, -1, 2) if (dx, dy) != (0, 0)],
+    key=lambda peer: -abs(peer[0]) - abs(peer[1]),
+)
+LINE_PEERS = (4, 3, 5, 2, 6, 1, 7)
 Z_STEPS = 7
 ROWS = 512
 ITEMS = (
@@ -307,11 +311,12 @@
 
     def advance(tile, item, done_tile, done_item):
         row = pl.multiple_of(ROWS + 8 * done_item[0], 8)
+        lasts = []
         for share in range(SHARES):
-            last = multiply(tile, item, share)
+            lasts.append(multiply(tile, item, share))
             accumulate(done_tile, done_item, share)
-            if share < SHARES - 1:
-                done_tile[pl.ds(row, 8), pl.ds(0, LANES)] = last
+            if 0 < share < SHARES - 1:
+                done_tile[pl.ds(row, 8), pl.ds(0, LANES)] = lasts[share - 1]
 
     def keep_self_apart(tile):
         block = tile[pl.ds(0, 2 * PIECE), pl.ds(0, 2 * PIECE)]
@@ -416,14 +421,14 @@
 
     def line_copy(n, src):
         return remote(
-            plane_ref, line_hist.at[src], line_send.at[n], line_recv.at[n], at(dz=n + 1)
+            plane_ref, line_hist.at[src], line_send.at[n], line_recv.at[n], at(dz=LINE_PEERS[n])
         )
 
     for n in range(7):
         line_copy(n, z).start()
     line_hist[z] = plane_ref[...]
     for n in range(7):
-        line_copy(n, lax.rem(z + (7 - n), 8)).wait_recv()
+        line_copy(n, lax.rem(z + (8 - LINE_PEERS[n]), 8)).wait_recv()
     line_ref[...] = tree_sum([line_hist[i] for i in range(8)])
     last = remote(line_ref, core_hist, last_send, last_recv, at(dc=1))
     last.start()

time: 65.9 us -> 64.4 us (0.977)
  Pallas kernels: 62.6 us -> 61.1 us
    pallas_call x1, Pallas kernels: 62.6 us -> 61.1 us  [on_device(): pl.pallas_call(functools.partial(kernel, math.log(total_genes), samples),...]
where the time goes in v4:
time: 64.4 us; the launch traced here: 64.1 us
  Pallas kernels  61.1 us (95%)
  local copies, waits for them, and re-layouts  2.43 us (4%)
  between operations  0.65 us (1%)
    pallas_call x1, Pallas kernels, on_device(): pl.pallas_call(functools.partial(kernel, math.log(total_genes), samples),...  61.1 us
    unnamed x7, local copies, waits for them, and re-layouts  2.43 us

profile of v4, /device:TPU:1, one launch (start us, length us, event | category | flops | bytes accessed | tf_op | source)
XLA Modules:
  0.0 64.1 jit_solution(2739915380166633480)
XLA Ops:
  0.6 61.1 %coexpression.1 = (f32[20,128]{1,0:T(8,128)}, f32[1,20]{1,0:T(1,128)}, f32[1,20]{1,0:T(1,128)}) custom-call(bf16[128,1024]{1,0:T(8,128)(2,1)} %x_ref.1, s32[20]{0:T(128)} %order_ref.1), custom_call_target="tpu_custom_call" | custom-call | tf_op jit(solution)/shard_map/coexpression/pallas_call | solution.py:483
  61.7 0.0 copy-start.1
  61.7 1.3 %copy.8 = f32[128,20]{0,1:T(8,128)} copy(f32[128,20]{0,1:T(8,128)} %bitcast.3) | data formatting | bytes 20480
  63.0 0.0 copy-done.1
  63.0 0.0 copy-start
  63.0 0.5 copy.9
  63.5 0.1 copy-done
  63.6 0.5 copy.10
Async XLA Ops:
  61.7 1.3 %copy-start.1 = (f32[1,20]{1,0:T(1,128)S(1)}, f32[1,20]{1,0:T(1,128)}, u32[]{:S(2)}) copy-start(f32[1,20]{1,0:T(1,128)} %get-tuple-element.7) | copy-start | bytes 244
  63.0 0.6 copy-start

commit v5 on v4

--- a/solution.py
+++ b/solution.py
@@ -315,8 +315,10 @@
         for share in range(SHARES):
             lasts.append(multiply(tile, item, share))
             accumulate(done_tile, done_item, share)
-            if 0 < share < SHARES - 1:
-                done_tile[pl.ds(row, 8), pl.ds(0, LANES)] = lasts[share - 1]
+            if share == 0:
+                done_tile[pl.ds(row, 8), pl.ds(0, LANES)] = lasts[0]
+            if share == SHARES - 2:
+                done_tile[pl.ds(row, 8), pl.ds(0, LANES)] = lasts[1]
 
     def keep_self_apart(tile):
         block = tile[pl.ds(0, 2 * PIECE), pl.ds(0, 2 * PIECE)]

time: 64.4 us -> 63.9 us (level)
  no operation moved by 1% of the time
where the time goes in v5:
time: 63.9 us; the launch traced here: 63.7 us
  Pallas kernels  60.6 us (95%)
  local copies, waits for them, and re-layouts  2.43 us (4%)
  between operations  0.65 us (1%)
    pallas_call x1, Pallas kernels, on_device(): pl.pallas_call(functools.partial(kernel, math.log(total_genes), samples),...  60.6 us
    unnamed x7, local copies, waits for them, and re-layouts  2.43 us

profile of v5, /device:TPU:1, one launch (start us, length us, event | category | flops | bytes accessed | tf_op | source)
XLA Modules:
  0.0 63.7 jit_solution(15698315861392648144)
XLA Ops:
  0.6 60.6 %coexpression.1 = (f32[20,128]{1,0:T(8,128)}, f32[1,20]{1,0:T(1,128)}, f32[1,20]{1,0:T(1,128)}) custom-call(bf16[128,1024]{1,0:T(8,128)(2,1)} %x_ref.1, s32[20]{0:T(128)} %order_ref.1), custom_call_target="tpu_custom_call" | custom-call | tf_op jit(solution)/shard_map/coexpression/pallas_call | solution.py:485
  61.3 0.0 copy-start.1
  61.3 1.3 %copy.8 = f32[128,20]{0,1:T(8,128)} copy(f32[128,20]{0,1:T(8,128)} %bitcast.3) | data formatting | bytes 20480
  62.6 0.0 copy-done.1
  62.6 0.0 copy-start
  62.6 0.5 copy.9
  63.1 0.1 copy-done
  63.2 0.5 copy.10
Async XLA Ops:
  61.3 1.3 %copy-start.1 = (f32[1,20]{1,0:T(1,128)S(1)}, f32[1,20]{1,0:T(1,128)}, u32[]{:S(2)}) copy-start(f32[1,20]{1,0:T(1,128)} %get-tuple-element.7) | copy-start | bytes 244
  62.6 0.6 copy-start

commit v6 on v5

--- a/solution.py
+++ b/solution.py
@@ -191,7 +191,7 @@
                 x_ref.at[:, cols], partners.at[k, pl.ds(0, 2 * PIECE), :], local_sem.at[1, k]
             )
         )
-    for copy in loads:
+    for copy in loads[::2] + loads[1::2]:
         copy.start()
 
     barrier = pltpu.get_barrier_semaphore()
@@ -199,7 +199,7 @@
     for device in near:
         pl.semaphore_signal(barrier, inc=1, device_id=device, device_id_type=MESH_ID)
     acc[...] = jnp.zeros_like(acc)
-    for copy in loads:
+    for copy in loads[::2]:
         copy.wait()
     pl.semaphore_wait(barrier, len(near))
 
@@ -260,6 +260,9 @@
                     z_copy(direction, step).wait_recv()
         for send in PLANE_SENDS[step]:
             plane_copy(*send).start()
+        if step == 0:
+            for copy in loads[1::2]:
+                copy.wait()
         for later in (1, 2) if step == 0 else (step + 2,):
             if later <= Z_STEPS:
                 for direction in (1, -1):

time: 63.9 us -> 63.9 us (level)
  no operation moved by 1% of the time
where the time goes in v6:
time: 63.9 us; the launch traced here: 63.7 us
  Pallas kernels  60.6 us (95%)
  local copies, waits for them, and re-layouts  2.43 us (4%)
  between operations  0.65 us (1%)
    pallas_call x1, Pallas kernels, on_device(): pl.pallas_call(functools.partial(kernel, math.log(total_genes), samples),...  60.6 us
    unnamed x7, local copies, waits for them, and re-layouts  2.43 us

profile of v6, /device:TPU:1, one launch (start us, length us, event | category | flops | bytes accessed | tf_op | source)
XLA Modules:
  0.0 63.7 jit_solution(3903500177308517804)
XLA Ops:
  0.6 60.6 %coexpression.1 = (f32[20,128]{1,0:T(8,128)}, f32[1,20]{1,0:T(1,128)}, f32[1,20]{1,0:T(1,128)}) custom-call(bf16[128,1024]{1,0:T(8,128)(2,1)} %x_ref.1, s32[20]{0:T(128)} %order_ref.1), custom_call_target="tpu_custom_call" | custom-call | tf_op jit(solution)/shard_map/coexpression/pallas_call | solution.py:488
  61.3 0.0 copy-start.1
  61.3 1.3 %copy.8 = f32[128,20]{0,1:T(8,128)} copy(f32[128,20]{0,1:T(8,128)} %bitcast.3) | data formatting | bytes 20480
  62.6 0.0 copy-done.1
  62.6 0.0 copy-start
  62.6 0.5 copy.9
  63.1 0.1 copy-done
  63.2 0.5 copy.10
Async XLA Ops:
  61.3 1.3 %copy-start.1 = (f32[1,20]{1,0:T(1,128)S(1)}, f32[1,20]{1,0:T(1,128)}, u32[]{:S(2)}) copy-start(f32[1,20]{1,0:T(1,128)} %get-tuple-element.7) | copy-start | bytes 244
  62.6 0.6 copy-start
